TPU v7x, 32 devices: a whole 2x2x4 slice. The times are simulated.
32 devices in a mesh: dir: 4 (over x, core), chan: 8 (over z, y).
Axes of the slice: x: 2, y: 2, z: 4, core: 2. Of those that a mesh axis runs over, the one named last changes fastest.
Arguments:
- visibilities: float32 [8, 256, 2, 256], P('chan'), may hold values from -4 to 4, as said below
- station_uv: float32 [2, 256], replicated, may hold values from -50 to 50
- source_lm: float32 [2, 64, 32], P(None, 'dir'), may hold values from -0.1 to 0.1
- source_flux: float32 [64, 32], P('dir'), may hold values from 0.01 to 0.1
- band_offset: float32 [8], P('chan'), may hold values from -1 to 1, as said below
- gains_init: float32 [2, 64, 8, 256], P(None, 'dir', 'chan'), may hold values from -1 to 2
- duals_init: float32 [2, 64, 8, 256], P(None, 'dir', 'chan'), may hold values from -3 to 3
- poly_init: float32 [2, 64, 1024], P(None, 'dir'), may hold values from -3 to 3
- penalty: float32 [64], P('dir'), may hold values from 1 to 8
- harmonics: float32 [64, 225], replicated, may hold values from -0.75 to 0.75
- threshold: float32 [1], replicated, may hold values from 0.1 to 0.4
Outputs:
- gains_new: float32 [2, 64, 8, 256], P(None, 'dir', 'chan')
- duals_new: float32 [2, 64, 8, 256], P(None, 'dir', 'chan')
- consensus: float32 [2, 64, 1024], P(None, 'dir')
Inputs may be any that keep to these rules, and one draw needn't show every extreme that they name: visibilities[c, p, 0, q] = visibilities[c, q, 0, p] and visibilities[c, p, 1, q] = -visibilities[c, q, 1, p]. `band_offset`: strictly increasing.
All inputs are finite; a program needn't handle non-finite values.
Results may differ from a plain program's by a relative error of at most 0.0003.
Values sent between devices are 32-bit elements; how exact they have to be, the bound alone decides.
A program may use at most 64 MiB of HBM per device.

v0:
```python
import functools
import math

import jax
import jax.numpy as jnp
import numpy as np
from jax import lax
from jax.experimental import pallas as pl
from jax.experimental.pallas import tpu as pltpu
from jax.sharding import PartitionSpec as P

NTERM = 4
SWEEPS = 2
MESH = pl.DeviceIdType.MESH
highest = lax.Precision.HIGHEST
VM = pl.BlockSpec(memory_space=pltpu.VMEM)


def fit_circle():
    nodes = np.cos(np.pi * (np.arange(400) + 0.5) / 800.0) * 0.5
    square = nodes * nodes
    scale = 0.25
    sine = np.polynomial.chebyshev.Chebyshev.fit(
        square, np.sin(2 * np.pi * nodes) / nodes, 5, domain=[0, scale], w=nodes
    ).convert(kind=np.polynomial.Polynomial)
    cosine = np.polynomial.chebyshev.Chebyshev.fit(
        square, np.cos(2 * np.pi * nodes), 6, domain=[0, scale]
    ).convert(kind=np.polynomial.Polynomial)
    return [float(c) for c in sine.coef], [float(c) for c in cosine.coef]


SINE, COSINE = fit_circle()


def horner(coefs, x):
    total = coefs[-1] * x + coefs[-2]
    for c in coefs[-3::-1]:
        total = total * x + c
    return total


def circle(turns):
    r = turns - jnp.round(turns)
    square = r * r
    return horner(COSINE, square), r * horner(SINE, square)


def legendre(x):
    return [
        jnp.ones_like(x),
        x,
        0.5 * (3.0 * x * x - 1.0),
        0.5 * (5.0 * x * x * x - 3.0 * x),
    ]


def split(x):
    high = x.astype(jnp.bfloat16)
    low = (x - high.astype(jnp.float32)).astype(jnp.bfloat16)
    return high, low


def tdot(a, b):
    return lax.dot_general(a, b, (((0,), (0,)), ((), ())), preferred_element_type=jnp.float32)


def meet(n_dir, n_chan, me_d, me_c):
    barrier = pltpu.get_barrier_semaphore()
    for j in range(1, n_dir):
        pl.semaphore_signal(
            barrier, inc=1, device_id={"dir": lax.rem(me_d + j, n_dir)}, device_id_type=MESH
        )
    for j in range(1, n_chan):
        pl.semaphore_signal(
            barrier, inc=1, device_id={"chan": lax.rem(me_c + j, n_chan)}, device_id_type=MESH
        )
    pl.semaphore_wait(barrier, n_dir + n_chan - 2)


def gather_kernel(
    n_dir, n_chan, g_ref, s_ref, b_ref, g_all, s_all, b_all, gs, gr, ss, sr, bs, br
):
    me_d, me_c = lax.axis_index("dir"), lax.axis_index("chan")
    meet(n_dir, n_chan, me_d, me_c)
    copies = []
    for j in range(1, n_dir):
        peer = {"dir": lax.rem(me_d + n_dir - j, n_dir)}
        for src, dst, a, b in ((g_ref, g_all, gs, gr), (s_ref, s_all, ss, sr)):
            copies.append(
                pltpu.make_async_remote_copy(
                    src_ref=src,
                    dst_ref=dst.at[j],
                    send_sem=a.at[j],
                    recv_sem=b.at[j],
                    device_id=peer,
                    device_id_type=MESH,
                )
            )
    for j in range(1, n_chan):
        peer = {"chan": lax.rem(me_c + n_chan - j, n_chan)}
        copies.append(
            pltpu.make_async_remote_copy(
                src_ref=b_ref,
                dst_ref=b_all.at[j],
                send_sem=bs.at[j],
                recv_sem=br.at[j],
                device_id=peer,
                device_id_type=MESH,
            )
        )
    for c in copies:
        c.start()
    g_all[0] = g_ref[...]
    s_all[0] = s_ref[...]
    b_all[0] = b_ref[...]
    for c in copies:
        c.wait()


def solve_kernel(
    n_dir,
    n_chan,
    sources,
    b_all,
    uv,
    g_all,
    s_all,
    vis,
    dual,
    poly,
    pen,
    gains,
    zout,
    src_t,
    er,
    ei,
    macc,
    rows,
):
    pair, stations = dual.shape
    clusters = pair // 2
    here = b_all[0, 0:1, 0:1]
    stretch = 1.0 + 0.25 * here
    u = uv[0:1, :] * stretch
    v = uv[1:2, :] * stretch
    chunk = math.gcd(clusters, 4)
    chunks = clusters // chunk
    span = chunk * sources
    macc[...] = jnp.zeros_like(macc)

    def step(d, c, keep):
        start = pl.multiple_of(c * span, span)
        cols = src_t[pl.ds(start, span), :]
        weight = cols[:, 2:3]
        e_r, e_i = circle(cols[:, 0:1] * u + cols[:, 1:2] * v)
        if keep:
            er[pl.ds(start, span), :] = e_r
            ei[pl.ds(start, span), :] = e_i
        f_r, f_i = [], []
        for i in range(chunk):
            a = g_all[d, pl.ds(c * chunk + i, 1), :]
            b = g_all[d, pl.ds(clusters + c * chunk + i, 1), :]
            part_r = e_r[i * sources : (i + 1) * sources]
            part_i = e_i[i * sources : (i + 1) * sources]
            f_r.append(part_r * a - part_i * b)
            f_i.append(part_r * b + part_i * a)
        f_r = jnp.concatenate(f_r, axis=0)
        f_i = jnp.concatenate(f_i, axis=0)
        left = jnp.concatenate([f_r * weight, f_i * weight], axis=0)
        lh, ll = split(left)
        rh, rl = split(f_r)
        ih, il = split(f_i)
        high = jnp.concatenate(
            [jnp.concatenate([rh, ih], axis=0), jnp.concatenate([-ih, rh], axis=0)], axis=1
        )
        low = jnp.concatenate(
            [jnp.concatenate([rl, il], axis=0), jnp.concatenate([-il, rl], axis=0)], axis=1
        )
        macc[...] += tdot(lh, high) + (tdot(lh, low) + tdot(ll, high))

    def others(d, carry):
        src_t[...] = jnp.transpose(s_all[d])
        lax.fori_loop(0, chunks, lambda c, x: (step(d, c, False), x)[1], 0)
        return carry

    lax.fori_loop(1, n_dir, others, 0)
    src_t[...] = jnp.transpose(s_all[0])
    lax.fori_loop(0, chunks, lambda c, x: (step(0, c, True), x)[1], 0)
    macc[:, :stations] = vis[0] - macc[:, :stations]
    macc[:, stations:] = vis[1] - macc[:, stations:]

    level = legendre(here)
    row = lax.broadcasted_iota(jnp.int32, (stations * NTERM, stations), 0)
    col = lax.broadcasted_iota(jnp.int32, (stations * NTERM, stations), 1)
    rest = row - NTERM * col
    pick = jnp.zeros((stations * NTERM, stations), jnp.float32)
    for t in range(NTERM):
        pick = jnp.where(rest == t, level[t], pick)
    pull = jnp.concatenate([pen[...], pen[...]], axis=0)
    offset = dual[...] / pull
    target = jnp.dot(poly[...], pick, precision=highest) - offset
    goal = target * pull
    for k in range(clusters):
        rows[k, 0:1, :] = g_all[0, k : k + 1, :]
        rows[k, 1:2, :] = g_all[0, clusters + k : clusters + k + 1, :]
        rows[k, 2:3, :] = goal[k : k + 1]
        rows[k, 3:4, :] = goal[clusters + k : clusters + k + 1]
        rows[k, 4:5, :] = jnp.broadcast_to(pen[k : k + 1, :], (1, stations))
        rows[k, 5:8, :] = jnp.zeros((3, stations), jnp.float32)

    def solve(k, carry):
        start = pl.multiple_of(k * sources, sources)
        e_r = er[pl.ds(start, sources), :]
        e_i = ei[pl.ds(start, sources), :]
        weight = src_t[pl.ds(start, sources), :][:, 2:3]
        lh, ll = split(jnp.concatenate([e_r * weight, e_i * weight], axis=0))
        rh, rl = split(
            jnp.concatenate(
                [jnp.concatenate([e_r, e_i], axis=0), jnp.concatenate([-e_i, e_r], axis=0)],
                axis=1,
            )
        )
        coherency = tdot(
            jnp.concatenate([lh, lh, ll], axis=0), jnp.concatenate([rh, rl, rh], axis=0)
        )
        c_r = coherency[:, :stations]
        c_i = coherency[:, stations:]
        r_r = macc[:, :stations]
        r_i = macc[:, stations:]
        power = c_r * c_r + c_i * c_i
        b_r = r_r * c_r + r_i * c_i
        b_i = r_i * c_r - r_r * c_i
        block = rows[k]
        g_r, g_i = block[0:1], block[1:2]
        cols = jnp.transpose(block)
        k_r, k_i = cols[:, 0:1], cols[:, 1:2]
        rho = cols[:, 4:5]
        n_r = jnp.sum(b_r * g_r - b_i * g_i, axis=1, keepdims=True)
        n_i = jnp.sum(b_r * g_i + b_i * g_r, axis=1, keepdims=True)
        total = jnp.sum(power * (g_r * g_r + g_i * g_i), axis=1, keepdims=True)
        inverse = 1.0 / (total + rho)
        h_r = (n_r + k_r * total + cols[:, 2:3]) * inverse
        h_i = (n_i + k_i * total + cols[:, 3:4]) * inverse
        mix_r = k_r * h_r + k_i * h_i
        mix_i = k_r * h_i - k_i * h_r
        m_r = jnp.sum(b_r * h_r + b_i * h_i, axis=0, keepdims=True)
        m_i = jnp.sum(b_r * h_i - b_i * h_r, axis=0, keepdims=True)
        t_0 = jnp.sum(power * mix_r, axis=0, keepdims=True)
        t_1 = jnp.sum(power * mix_i, axis=0, keepdims=True)
        t_2 = jnp.sum(power * (h_r * h_r + h_i * h_i), axis=0, keepdims=True)
        inverse = 1.0 / (t_2 + block[4:5])
        gains[pl.ds(k, 1), :] = (m_r + g_r * t_0 - g_i * t_1 + block[2:3]) * inverse
        gains[pl.ds(clusters + k, 1), :] = (m_i + g_r * t_1 + g_i * t_0 + block[3:4]) * inverse
        return carry

    lax.fori_loop(0, clusters, solve, 0)

    values = legendre(b_all[:, 0, :])
    gram = [
        [jnp.sum(values[t] * values[s], axis=0, keepdims=True) for s in range(t + 1)]
        for t in range(NTERM)
    ]
    factor = [[None] * NTERM for _ in range(NTERM)]
    for t in range(NTERM):
        for s in range(t + 1):
            rest_sum = gram[t][s]
            for r in range(s):
                rest_sum = rest_sum - factor[t][r] * factor[s][r]
            factor[t][s] = jnp.sqrt(rest_sum) if s == t else rest_sum / factor[s][s]
    mine = legendre(b_all[0, 0:1, :])
    half = []
    for t in range(NTERM):
        rest_sum = mine[t]
        for s in range(t):
            rest_sum = rest_sum - factor[t][s] * half[s]
        half.append(rest_sum / factor[t][t])
    taps = [None] * NTERM
    for t in reversed(range(NTERM)):
        rest_sum = half[t]
        for s in range(t + 1, NTERM):
            rest_sum = rest_sum - factor[s][t] * taps[s]
        taps[t] = rest_sum / factor[t][t]
    row = lax.broadcasted_iota(jnp.int32, (stations, stations * NTERM), 0)
    col = lax.broadcasted_iota(jnp.int32, (stations, stations * NTERM), 1)
    rest = col - NTERM * row
    spread_out = jnp.zeros((stations, stations * NTERM), jnp.float32)
    for t in range(NTERM):
        spread_out = jnp.where(rest == t, taps[t][:, 0:1], spread_out)
    z = jnp.dot(gains[...] + offset, spread_out, precision=highest)
    width = stations * NTERM // n_chan
    for j in range(n_chan):
        if width < zout.shape[2]:
            zout[j] = jnp.zeros(zout.shape[1:], jnp.float32)
        zout[j, :, :width] = z[:, j * width : (j + 1) * width]


def smooth_kernel(
    n_dir, n_chan, z_ref, harm, cut, out, zin, own, zall, part, s1, r1, s2, r2, s3, r3
):
    me_d, me_c = lax.axis_index("dir"), lax.axis_index("chan")
    meet(n_dir, n_chan, me_d, me_c)
    pair = own.shape[0]
    clusters = pair // 2

    def send(src, dst, a, b, peer):
        return pltpu.make_async_remote_copy(
            src_ref=src, dst_ref=dst, send_sem=a, recv_sem=b, device_id=peer, device_id_type=MESH
        )

    first = []
    for j in range(1, n_chan):
        peer = lax.rem(me_c + j, n_chan)
        first.append(send(z_ref.at[peer], zin.at[j], s1.at[j], r1.at[j], {"chan": peer}))
    for c in first:
        c.start()
    total = z_ref[me_c]
    for j, c in enumerate(first):
        c.wait_recv()
        total = total + zin[j + 1]
    own[...] = total
    second = []
    for j in range(1, n_dir):
        peer = lax.rem(me_d + j, n_dir)
        second.append(send(own, zall.at[me_d], s2.at[j], r2.at[j], {"dir": peer}))
    for c in second:
        c.start()
    zall[me_d] = total
    for c in second:
        c.wait()
    coeff_r = jnp.concatenate([zall[d][:clusters] for d in range(n_dir)], axis=0)
    coeff_i = jnp.concatenate([zall[d][clusters:] for d in range(n_dir)], axis=0)
    both = jnp.concatenate([coeff_r, coeff_i], axis=1)
    lanes = own.shape[1]
    a = lax.dot_general(
        harm[...],
        both,
        (((0,), (0,)), ((), ())),
        precision=highest,
        preferred_element_type=jnp.float32,
    )
    a_r, a_i = a[:, :lanes], a[:, lanes:]
    size = jnp.sqrt(a_r * a_r + a_i * a_i)
    limit = cut[0:1, 0:1]
    scale = jnp.maximum(size - limit, 0.0) / jnp.maximum(size, limit)
    mine = harm[pl.ds(pl.multiple_of(me_d * clusters, clusters), clusters), :]
    done = jnp.dot(
        mine, jnp.concatenate([a_r * scale, a_i * scale], axis=1), precision=highest
    )
    part[:clusters] = done[:, :lanes]
    part[clusters:] = done[:, lanes:]
    third = []
    for j in range(1, n_chan):
        peer = lax.rem(me_c + j, n_chan)
        third.append(send(part, out.at[me_c], s3.at[j], r3.at[j], {"chan": peer}))
    for c in third:
        c.start()
    out[me_c] = part[...]
    for c in third:
        c.wait()
    for c in first:
        c.wait_send()


def finish_kernel(n_chan, blocks, band, gains, dual, pen, cons_out, dual_out):
    pair, stations = gains.shape
    width = stations * NTERM // n_chan
    level = legendre(band[0:1, 0:1])
    for j in range(n_chan):
        cons_out[:, j * width : (j + 1) * width] = blocks[j][:, :width]
    row = lax.broadcasted_iota(jnp.int32, (stations * NTERM, stations), 0)
    col = lax.broadcasted_iota(jnp.int32, (stations * NTERM, stations), 1)
    rest = row - NTERM * col
    pick = jnp.zeros((stations * NTERM, stations), jnp.float32)
    for t in range(NTERM):
        pick = jnp.where(rest == t, level[t], pick)
    fitted = jnp.dot(cons_out[...], pick, precision=highest)
    pull = jnp.concatenate([pen[...], pen[...]], axis=0)
    dual_out[...] = dual[...] + pull * (gains[...] - fitted)


def solution(mesh):
    n_dir, n_chan = mesh.shape["dir"], mesh.shape["chan"]

    def shards(
        visibilities,
        station_uv,
        source_lm,
        source_flux,
        band_offset,
        gains_init,
        duals_init,
        poly_init,
        penalty,
        harmonics,
        threshold,
    ):
        f32 = jnp.float32
        _, clusters, sources = source_lm.shape
        stations = station_uv.shape[1]
        pair = 2 * clusters
        lanes = max(128, stations * NTERM // n_chan)
        g0 = gains_init.reshape(pair, stations)
        dual = duals_init.reshape(pair, stations)
        poly = poly_init.reshape(pair, stations * NTERM)
        flat = clusters * sources
        table = jnp.concatenate(
            [
                source_lm.reshape(2, flat),
                source_flux.reshape(1, flat),
                jnp.zeros((5, flat), f32),
            ],
            axis=0,
        )
        band = jnp.broadcast_to(band_offset.reshape(1, 1), (8, 128))
        cut = jnp.broadcast_to(threshold.reshape(1, 1), (8, 128))
        pen = penalty.reshape(clusters, 1)
        vis = jnp.transpose(visibilities[0], (1, 0, 2))
        dma = pltpu.SemaphoreType.DMA
        g_all, s_all, b_all = pl.pallas_call(
            functools.partial(gather_kernel, n_dir, n_chan),
            out_shape=(
                jax.ShapeDtypeStruct((n_dir, pair, stations), f32),
                jax.ShapeDtypeStruct((n_dir, 8, flat), f32),
                jax.ShapeDtypeStruct((n_chan, 8, 128), f32),
            ),
            in_specs=[VM] * 3,
            out_specs=(VM,) * 3,
            scratch_shapes=[
                dma((n_dir,)),
                dma((n_dir,)),
                dma((n_dir,)),
                dma((n_dir,)),
                dma((n_chan,)),
                dma((n_chan,)),
            ],
            compiler_params=pltpu.CompilerParams(collective_id=0, has_side_effects=True),
            name="gather_inputs",
        )(g0, table, band)
        gains, z = pl.pallas_call(
            functools.partial(solve_kernel, n_dir, n_chan, sources),
            out_shape=(
                jax.ShapeDtypeStruct((pair, stations), f32),
                jax.ShapeDtypeStruct((n_chan, pair, lanes), f32),
            ),
            in_specs=[VM] * 8,
            out_specs=(VM,) * 2,
            scratch_shapes=[
                pltpu.VMEM((flat, 8), f32),
                pltpu.VMEM((flat, stations), f32),
                pltpu.VMEM((flat, stations), f32),
                pltpu.VMEM((stations, 2 * stations), f32),
                pltpu.VMEM((clusters, 8, stations), f32),
            ],
            name="solve_gains",
        )(b_all, station_uv, g_all, s_all, vis, dual, poly, pen)
        blocks = pl.pallas_call(
            functools.partial(smooth_kernel, n_dir, n_chan),
            out_shape=jax.ShapeDtypeStruct((n_chan, pair, lanes), f32),
            in_specs=[VM] * 3,
            out_specs=VM,
            scratch_shapes=[
                pltpu.VMEM((n_chan, pair, lanes), f32),
                pltpu.VMEM((pair, lanes), f32),
                pltpu.VMEM((n_dir, pair, lanes), f32),
                pltpu.VMEM((pair, lanes), f32),
                dma((n_chan,)),
                dma((n_chan,)),
                dma((n_dir,)),
                dma((n_dir,)),
                dma((n_chan,)),
                dma((n_chan,)),
            ],
            compiler_params=pltpu.CompilerParams(collective_id=1, has_side_effects=True),
            name="smooth",
        )(z, harmonics, cut)
        consensus, duals = pl.pallas_call(
            functools.partial(finish_kernel, n_chan),
            out_shape=(
                jax.ShapeDtypeStruct((pair, stations * NTERM), f32),
                jax.ShapeDtypeStruct((pair, stations), f32),
            ),
            in_specs=[VM] * 5,
            out_specs=(VM,) * 2,
            name="finish",
        )(blocks, band, gains, dual, pen)
        shape = (2, clusters, 1, stations)
        return (
            gains.reshape(shape),
            duals.reshape(shape),
            consensus.reshape(2, clusters, stations * NTERM),
        )

    return jax.shard_map(
        shards,
        mesh=mesh,
        in_specs=(
            P("chan", None, None, None),
            P(),
            P(None, "dir", None),
            P("dir", None),
            P("chan"),
            P(None, "dir", "chan", None),
            P(None, "dir", "chan", None),
            P(None, "dir", None),
            P("dir"),
            P(),
            P(),
        ),
        out_specs=(
            P(None, "dir", "chan", None),
            P(None, "dir", "chan", None),
            P(None, "dir", None),
        ),
        check_vma=False,
    )
```

profile of v0, /device:TPU:0, one launch (start us, length us, event | category | flops | bytes accessed | tf_op | source)
XLA Modules:
  0.0 75.5 jit_solution(17632600676430002569)
XLA Ops:
  1.3 0.6 broadcast_in_dim.19.b_ref.band
  1.9 0.0 copy-start.2
  1.9 1.4 %copy.19 = f32[2,16,1,256]{3,1,2,0:T(8,128)} copy(f32[2,16,1,256]{3,2,1,0:T(1,128)} %param.16) | data formatting | bytes 65536
  3.3 0.0 copy-done.2
  3.3 0.0 copy-start.3
  3.3 0.1 reshape.38
  3.3 0.6 copy-done.3
  4.0 0.1 reshape.39
  4.0 0.1 pad.2.clone
  4.1 0.7 maximum_maximum_fusion.s_ref
  4.8 0.0 copy-start.1
  4.8 11.9 %gather_inputs.1 = (f32[4,32,256]{2,1,0:T(8,128)}, f32[4,8,512]{2,1,0:T(8,128)}, f32[8,8,128]{2,1,0:T(8,128)}) custom-call(f32[32,256]{1,0:T(8,128)} %bitcast.21, f32[8,512]{1,0:T(8,128)} %maximum_maximum_fusion.s_ref, f32[8,128]{1,0:T(8,128)} %broadcast_in_dim.19.b_ref.band), custom_call_target="tpu_custom_call" | custom-call | tf_op jit(solution)/shard_map/gather_inputs/pallas_call | solution.py:419
  16.7 0.0 copy-done.1
  16.7 0.6 copy.20
  17.3 0.7 copy-done.4
  18.0 0.7 copy.15.pen
  18.7 1.9 %copy.22 = f32[1,256,2,256]{3,1,2,0:T(8,128)} copy(f32[1,256,2,256]{3,2,1,0:T(2,128)} %param.11) | data formatting | bytes 1048576 | tf_op args[0]
  20.5 31.7 %solve_gains.1 = (f32[32,256]{1,0:T(8,128)}, f32[8,32,128]{2,1,0:T(8,128)}) custom-call(f32[8,8,128]{2,1,0:T(8,128)} %get-tuple-element.10.b_all, f32[2,256]{1,0:T(2,128)} %uv.1, f32[4,32,256]{2,1,0:T(8,128)} %get-tuple-element.11.g_all, f32[4,8,512]{2,1,0:T(8,128)} %get-tuple-element.12.s_all, f32[2,256,256]{2,1,0:T(8,128)} %bitcast.16, ...), custom_call_target="tpu_custom_call" | custom-call | tf_op jit(solution)/shard_map/solve_gains/pallas_call | solution.py:439
  52.9 0.6 broadcast_in_dim.21.cut
  53.4 17.5 %smooth.1.blocks = f32[8,32,128]{2,1,0:T(8,128)} custom-call(f32[8,32,128]{2,1,0:T(8,128)} %get-tuple-element.14.z_ref, f32[64,225]{1,0:T(8,128)} %harm.1, f32[8,128]{1,0:T(8,128)} %broadcast_in_dim.21.cut), custom_call_target="tpu_custom_call" | custom-call | tf_op jit(solution)/shard_map/smooth/pallas_call | solution.py:456
  70.9 2.5 %finish.1 = (f32[32,1024]{1,0:T(8,128)}, f32[32,256]{1,0:T(8,128)}) custom-call(f32[8,32,128]{2,1,0:T(8,128)} %smooth.1.blocks, f32[8,128]{1,0:T(8,128)} %broadcast_in_dim.19.b_ref.band, f32[32,256]{1,0:T(8,128)} %get-tuple-element.13.gains, f32[32,256]{1,0:T(8,128)} %bitcast.18, f32[16,1]{1,0:T(8,128)} %copy.15.pen), custom_call_target="tpu_custom_call" | custom-call | tf_op jit(solution)/shard_map/finish/pallas_call | solution.py:476
  73.4 1.4 %copy.18 = f32[2,16,1,256]{3,2,1,0:T(1,128)} copy(f32[2,16,1,256]{3,1,0,2:T(8,128)} %bitcast.22) | data formatting | bytes 65536
  74.9 0.0 copy-done
  74.9 0.6 copy.17
  (3 shorter events, 0.0 us)
Async XLA Ops:
  1.9 1.4 %copy-start.2 = (f32[2,16,32]{2,1,0:T(8,128)S(1)}, f32[2,16,32]{2,1,0:T(8,128)}, u32[]{:S(2)}) copy-start(f32[2,16,32]{2,1,0:T(8,128)} %param.13) | copy-start | bytes 12292
  3.3 0.7 copy-start.3
  4.8 11.9 %copy-start.1 = (f32[2,16,1,256]{3,2,1,0:T(1,128)S(1)}, f32[2,16,1,256]{3,2,1,0:T(1,128)}, u32[]{:S(2)}) copy-start(f32[2,16,1,256]{3,2,1,0:T(1,128)} %param.17) | copy-start | bytes 98308
  17.3 0.7 copy-start.4
  73.4 1.4 %copy-start = (f32[32,256]{1,0:T(8,128)S(1)}, f32[32,256]{1,0:T(8,128)}, u32[]{:S(2)}) copy-start(f32[32,256]{1,0:T(8,128)} %get-tuple-element.13.gains) | copy-start | bytes 98308
where the time goes:
time: 76 us; the launch traced here: 75.5 us
  Pallas kernels  63.6 us (84%)
  local copies, waits for them, and re-layouts  9.31 us (12%)
  between operations  1.96 us (3%)
    pallas_call x1, Pallas kernels, shards(): pl.pallas_call(functools.partial(solve_kernel, n_dir, n_chan, sources), o...  31.7 us
    pallas_call x1, Pallas kernels, shards(): pl.pallas_call(functools.partial(smooth_kernel, n_dir, n_chan), out_shape...  17.5 us
    pallas_call x1, Pallas kernels, shards(): pl.pallas_call(functools.partial(gather_kernel, n_dir, n_chan), out_shape...  11.9 us
    unnamed x15, local copies, waits for them, and re-layouts  7.22 us
    pallas_call x1, Pallas kernels, shards(): pl.pallas_call(functools.partial(finish_kernel, n_chan), out_shape=(jax.S...  2.51 us

commit v1 on v0

v1 whole, which is shorter than its diff:
```python
import functools
import math

import jax
import jax.numpy as jnp
import numpy as np
from jax import lax
from jax.experimental import pallas as pl
from jax.experimental.pallas import tpu as pltpu
from jax.sharding import PartitionSpec as P

NTERM = 4
SWEEPS = 2
MESH = pl.DeviceIdType.MESH
highest = lax.Precision.HIGHEST
VM = pl.BlockSpec(memory_space=pltpu.VMEM)


def fit_circle():
    nodes = np.cos(np.pi * (np.arange(400) + 0.5) / 800.0) * 0.5
    square = nodes * nodes
    scale = 0.25
    sine = np.polynomial.chebyshev.Chebyshev.fit(
        square, np.sin(2 * np.pi * nodes) / nodes, 5, domain=[0, scale], w=nodes
    ).convert(kind=np.polynomial.Polynomial)
    cosine = np.polynomial.chebyshev.Chebyshev.fit(
        square, np.cos(2 * np.pi * nodes), 6, domain=[0, scale]
    ).convert(kind=np.polynomial.Polynomial)
    return [float(c) for c in sine.coef], [float(c) for c in cosine.coef]


SINE, COSINE = fit_circle()


def horner(coefs, x):
    total = coefs[-1] * x + coefs[-2]
    for c in coefs[-3::-1]:
        total = total * x + c
    return total


def circle(turns):
    r = turns - jnp.round(turns)
    square = r * r
    return horner(COSINE, square), r * horner(SINE, square)


def legendre(x):
    return [
        jnp.ones_like(x),
        x,
        0.5 * (3.0 * x * x - 1.0),
        0.5 * (5.0 * x * x * x - 3.0 * x),
    ]


def split(x):
    high = x.astype(jnp.bfloat16)
    low = (x - high.astype(jnp.float32)).astype(jnp.bfloat16)
    return high, low


def tdot(a, b):
    return lax.dot_general(a, b, (((0,), (0,)), ((), ())), preferred_element_type=jnp.float32)


def meet(n_dir, n_chan, me_d, me_c):
    barrier = pltpu.get_barrier_semaphore()
    for j in range(1, n_dir):
        pl.semaphore_signal(
            barrier, inc=1, device_id={"dir": lax.rem(me_d + j, n_dir)}, device_id_type=MESH
        )
    for j in range(1, n_chan):
        pl.semaphore_signal(
            barrier, inc=1, device_id={"chan": lax.rem(me_c + j, n_chan)}, device_id_type=MESH
        )
    pl.semaphore_wait(barrier, n_dir + n_chan - 2)


def column(pen):
    count = pen.shape[1]
    row = lax.broadcasted_iota(jnp.int32, (count, count), 0)
    col = lax.broadcasted_iota(jnp.int32, (count, count), 1)
    return jnp.sum(jnp.where(row == col, pen[...], 0.0), axis=1, keepdims=True)


def step_kernel(
    n_dir,
    n_chan,
    sources,
    vis,
    uv,
    table,
    band,
    g_ref,
    dual_ref,
    poly,
    pen_ref,
    harm,
    cut,
    gains_out,
    dual_out,
    cons_out,
    b_ref,
    g_all,
    s_all,
    b_all,
    src_t,
    er,
    ei,
    macc,
    rows,
    dual,
    gains,
    packed,
    zin,
    own,
    zall,
    part,
    blocks,
    gs,
    gr,
    ss,
    sr,
    bs,
    br,
    s1,
    r1,
    s2,
    r2,
    s3,
    r3,
):
    pair, stations = dual.shape
    clusters = pair // 2
    me_d, me_c = lax.axis_index("dir"), lax.axis_index("chan")
    b_ref[...] = jnp.full(b_ref.shape, band[0], jnp.float32)

    def send(src, dst, a, b, peer):
        return pltpu.make_async_remote_copy(
            src_ref=src, dst_ref=dst, send_sem=a, recv_sem=b, device_id=peer, device_id_type=MESH
        )

    meet(n_dir, n_chan, me_d, me_c)
    copies = []
    for j in range(1, n_dir):
        peer = {"dir": lax.rem(me_d + n_dir - j, n_dir)}
        copies.append(send(g_ref, g_all.at[j], gs.at[j], gr.at[j], peer))
        copies.append(send(table, s_all.at[j], ss.at[j], sr.at[j], peer))
    for j in range(1, n_chan):
        peer = {"chan": lax.rem(me_c + n_chan - j, n_chan)}
        copies.append(send(b_ref, b_all.at[j], bs.at[j], br.at[j], peer))
    for c in copies:
        c.start()
    b_all[0] = b_ref[...]
    g_all[0] = g_ref[...]

    here = b_ref[0:1, 0:1]
    stretch = 1.0 + 0.25 * here
    u = uv[0:1, :] * stretch
    v = uv[1:2, :] * stretch
    chunk = math.gcd(clusters, 4)
    chunks = clusters // chunk
    span = chunk * sources
    macc[:, :stations] = jnp.zeros((stations, stations), jnp.float32)

    def step(d, c, keep):
        start = pl.multiple_of(c * span, span)
        cols = src_t[pl.ds(start, span), :]
        weight = cols[:, 2:3]
        e_r, e_i = circle(cols[:, 0:1] * u + cols[:, 1:2] * v)
        if keep:
            er[pl.ds(start, span), :] = e_r
            ei[pl.ds(start, span), :] = e_i
        f_r, f_i = [], []
        for i in range(chunk):
            a = g_all[d, 0, c * chunk + i]
            b = g_all[d, 1, c * chunk + i]
            part_r = e_r[i * sources : (i + 1) * sources]
            part_i = e_i[i * sources : (i + 1) * sources]
            f_r.append(part_r * a - part_i * b)
            f_i.append(part_r * b + part_i * a)
        f_r = jnp.concatenate(f_r, axis=0)
        f_i = jnp.concatenate(f_i, axis=0)
        lh, ll = split(jnp.concatenate([f_r * weight, f_i * weight], axis=0))
        high, low = split(jnp.concatenate([f_r - f_i, f_i + f_r], axis=0))
        macc[:, :stations] += tdot(lh, high) + (tdot(lh, low) + tdot(ll, high))

    src_t[...] = jnp.transpose(table[...])
    lax.fori_loop(0, chunks, lambda c, x: (step(0, c, True), x)[1], 0)

    for k in range(clusters):
        dual[k : k + 1, :] = dual_ref[0, k]
        dual[clusters + k : clusters + k + 1, :] = dual_ref[1, k]
    level = legendre(here)
    pen = column(pen_ref)
    pull = jnp.concatenate([pen, pen], axis=0)
    tile = 32 * NTERM
    tiles = stations // 32
    row = lax.broadcasted_iota(jnp.int32, (tile, tile), 0)
    col = lax.broadcasted_iota(jnp.int32, (tile, tile), 1)
    pick = jnp.zeros((tile, tile), jnp.float32)
    for t in range(NTERM):
        pick = jnp.where(row - NTERM * col == t, level[t], pick)
    stacked = jnp.concatenate([poly[:, j * tile : (j + 1) * tile] for j in range(tiles)], axis=0)
    value = jnp.dot(stacked, pick, precision=highest)
    value = jnp.concatenate(
        [value[j * pair : (j + 1) * pair, :32] for j in range(tiles)], axis=1
    )
    offset = dual[...] / pull
    goal = (value - offset) * pull
    for k in range(clusters):
        rows[k, 0:1, :] = g_ref[0, k]
        rows[k, 1:2, :] = g_ref[1, k]
        rows[k, 2:3, :] = goal[k : k + 1]
        rows[k, 3:4, :] = goal[clusters + k : clusters + k + 1]
        rows[k, 4:5, :] = jnp.broadcast_to(pen[k : k + 1, :], (1, stations))
        rows[k, 5:8, :] = jnp.zeros((3, stations), jnp.float32)

    for c in copies:
        c.wait()

    def others(d, carry):
        src_t[...] = jnp.transpose(s_all[d])
        lax.fori_loop(0, chunks, lambda c, x: (step(d, c, False), x)[1], 0)
        return carry

    lax.fori_loop(1, n_dir, others, 0)
    src_t[...] = jnp.transpose(table[...])
    both = macc[:, :stations]
    turned = jnp.transpose(both)
    macc[:, :stations] = vis[:, 0, :] - 0.5 * (both + turned)
    macc[:, stations:] = vis[:, 1, :] - 0.5 * (both - turned)

    def solve(k, carry):
        start = pl.multiple_of(k * sources, sources)
        e_r = er[pl.ds(start, sources), :]
        e_i = ei[pl.ds(start, sources), :]
        weight = src_t[pl.ds(start, sources), :][:, 2:3]
        lh, ll = split(jnp.concatenate([e_r * weight, e_i * weight], axis=0))
        rh, rl = split(
            jnp.concatenate(
                [jnp.concatenate([e_r, e_i], axis=0), jnp.concatenate([-e_i, e_r], axis=0)],
                axis=1,
            )
        )
        coherency = tdot(
            jnp.concatenate([lh, lh, ll], axis=0), jnp.concatenate([rh, rl, rh], axis=0)
        )
        c_r = coherency[:, :stations]
        c_i = coherency[:, stations:]
        r_r = macc[:, :stations]
        r_i = macc[:, stations:]
        power = c_r * c_r + c_i * c_i
        b_r = r_r * c_r + r_i * c_i
        b_i = r_i * c_r - r_r * c_i
        block = rows[k]
        g_r, g_i = block[0:1], block[1:2]
        cols = jnp.transpose(block)
        k_r, k_i = cols[:, 0:1], cols[:, 1:2]
        rho = cols[:, 4:5]
        n_r = jnp.sum(b_r * g_r - b_i * g_i, axis=1, keepdims=True)
        n_i = jnp.sum(b_r * g_i + b_i * g_r, axis=1, keepdims=True)
        total = jnp.sum(power * (g_r * g_r + g_i * g_i), axis=1, keepdims=True)
        inverse = 1.0 / (total + rho)
        h_r = (n_r + k_r * total + cols[:, 2:3]) * inverse
        h_i = (n_i + k_i * total + cols[:, 3:4]) * inverse
        mix_r = k_r * h_r + k_i * h_i
        mix_i = k_r * h_i - k_i * h_r
        m_r = jnp.sum(b_r * h_r + b_i * h_i, axis=0, keepdims=True)
        m_i = jnp.sum(b_r * h_i - b_i * h_r, axis=0, keepdims=True)
        t_0 = jnp.sum(power * mix_r, axis=0, keepdims=True)
        t_1 = jnp.sum(power * mix_i, axis=0, keepdims=True)
        t_2 = jnp.sum(power * (h_r * h_r + h_i * h_i), axis=0, keepdims=True)
        inverse = 1.0 / (t_2 + block[4:5])
        new_r = (m_r + g_r * t_0 - g_i * t_1 + block[2:3]) * inverse
        new_i = (m_i + g_r * t_1 + g_i * t_0 + block[3:4]) * inverse
        gains[pl.ds(k, 1), :] = new_r
        gains[pl.ds(clusters + k, 1), :] = new_i
        gains_out[0, k] = new_r
        gains_out[1, k] = new_i
        return carry

    lax.fori_loop(0, clusters, solve, 0)

    spread = gains[...] + offset
    each = stations // n_chan
    groups = pair // 8
    used = groups * each
    lanes = packed.shape[2]
    for j in range(n_chan):
        if used < lanes:
            packed[j] = jnp.zeros((8, lanes), jnp.float32)
        packed[j, :, :used] = jnp.concatenate(
            [spread[8 * g : 8 * g + 8, j * each : (j + 1) * each] for g in range(groups)], axis=1
        )

    first = []
    for j in range(1, n_chan):
        peer = lax.rem(me_c + n_chan - j, n_chan)
        first.append(send(packed.at[peer], zin.at[j], s1.at[j], r1.at[j], {"chan": peer}))
    for c in first:
        c.start()

    everywhere = b_all[:, 0, :]
    values = legendre(everywhere)
    gram = [
        [jnp.sum(values[t] * values[s], axis=0, keepdims=True) for s in range(t + 1)]
        for t in range(NTERM)
    ]
    factor = [[None] * NTERM for _ in range(NTERM)]
    for t in range(NTERM):
        for s in range(t + 1):
            rest_sum = gram[t][s]
            for r in range(s):
                rest_sum = rest_sum - factor[t][r] * factor[s][r]
            factor[t][s] = jnp.sqrt(rest_sum) if s == t else rest_sum / factor[s][s]
    half = []
    for t in range(NTERM):
        rest_sum = values[t]
        for s in range(t):
            rest_sum = rest_sum - factor[t][s] * half[s]
        half.append(rest_sum / factor[t][t])
    taps = [None] * NTERM
    for t in reversed(range(NTERM)):
        rest_sum = half[t]
        for s in range(t + 1, NTERM):
            rest_sum = rest_sum - factor[s][t] * taps[s]
        taps[t] = rest_sum / factor[t][t]

    mixed = [packed[me_c] * taps[t][0:1, 0:1] for t in range(NTERM)]
    for j in range(1, n_chan):
        first[j - 1].wait_recv()
        got = zin[j]
        for t in range(NTERM):
            mixed[t] = mixed[t] + got * taps[t][j : j + 1, 0:1]
    wide = NTERM * each
    if wide < own.shape[1]:
        own[...] = jnp.zeros_like(own)
    for g in range(groups):
        own[8 * g : 8 * g + 8, :wide] = jnp.concatenate(
            [mixed[t][:, g * each : (g + 1) * each] for t in range(NTERM)], axis=1
        )
    second = []
    for j in range(1, n_dir):
        peer = lax.rem(me_d + j, n_dir)
        second.append(send(own, zall.at[me_d], s2.at[j], r2.at[j], {"dir": peer}))
    for c in second:
        c.start()
    zall[me_d] = own[...]
    for c in second:
        c.wait()
    width = own.shape[1]
    coeff_r = jnp.concatenate([zall[d][:clusters] for d in range(n_dir)], axis=0)
    coeff_i = jnp.concatenate([zall[d][clusters:] for d in range(n_dir)], axis=0)
    a = lax.dot_general(
        harm[...],
        jnp.concatenate([coeff_r, coeff_i], axis=1),
        (((0,), (0,)), ((), ())),
        precision=highest,
        preferred_element_type=jnp.float32,
    )
    a_r, a_i = a[:, :width], a[:, width:]
    size = jnp.sqrt(a_r * a_r + a_i * a_i)
    limit = cut[0]
    scale = jnp.maximum(size - limit, 0.0) / jnp.maximum(size, limit)
    mine = harm[pl.ds(pl.multiple_of(me_d * clusters, clusters), clusters), :]
    done = jnp.dot(
        mine, jnp.concatenate([a_r * scale, a_i * scale], axis=1), precision=highest
    )
    part[:clusters] = done[:, :width]
    part[clusters:] = done[:, width:]
    third = []
    for j in range(1, n_chan):
        peer = lax.rem(me_c + j, n_chan)
        third.append(send(part, blocks.at[me_c], s3.at[j], r3.at[j], {"chan": peer}))
    for c in third:
        c.start()
    blocks[me_c] = part[...]
    row = lax.broadcasted_iota(jnp.int32, (width, width), 0)
    col = lax.broadcasted_iota(jnp.int32, (width, width), 1)
    weave = jnp.zeros((width, width), jnp.float32)
    sample = jnp.zeros((width, width), jnp.float32)
    for t in range(NTERM):
        place = row - t * each
        inside = (place >= 0) & (place < each)
        weave = jnp.where(inside & (col == NTERM * place + t), 1.0, weave)
        sample = jnp.where(inside & (col == place), level[t], sample)
    for c in first:
        c.wait_send()
    for c in third:
        c.wait()
    result = jnp.dot(
        jnp.concatenate([blocks[j] for j in range(n_chan)], axis=0),
        jnp.concatenate([weave, sample], axis=1),
        precision=highest,
    )
    fitted = []
    for j in range(n_chan):
        piece = result[j * pair : (j + 1) * pair]
        cons_out[:, j * wide : (j + 1) * wide] = piece[:, :wide]
        fitted.append(piece[:, width : width + each])
    fitted = jnp.concatenate(fitted, axis=1)
    fresh = dual[...] + pull * (gains[...] - fitted)
    for k in range(clusters):
        dual_out[0, k] = fresh[k : k + 1]
        dual_out[1, k] = fresh[clusters + k : clusters + k + 1]


def solution(mesh):
    n_dir, n_chan = mesh.shape["dir"], mesh.shape["chan"]

    def shards(
        visibilities,
        station_uv,
        source_lm,
        source_flux,
        band_offset,
        gains_init,
        duals_init,
        poly_init,
        penalty,
        harmonics,
        threshold,
    ):
        f32 = jnp.float32
        _, clusters, sources = source_lm.shape
        stations = station_uv.shape[1]
        pair = 2 * clusters
        lanes = max(128, stations * NTERM // n_chan)
        poly = poly_init.reshape(pair, stations * NTERM)
        flat = clusters * sources
        table = jnp.concatenate(
            [
                source_lm.reshape(2, flat),
                source_flux.reshape(1, flat),
                jnp.zeros((5, flat), f32),
            ],
            axis=0,
        )
        dma = pltpu.SemaphoreType.DMA
        shape = (2, clusters, 1, stations)
        small = max(128, stations // n_chan * (pair // 8))
        SM = pl.BlockSpec(memory_space=pltpu.SMEM)
        gains, duals, consensus = pl.pallas_call(
            functools.partial(step_kernel, n_dir, n_chan, sources),
            out_shape=(
                jax.ShapeDtypeStruct(shape, f32),
                jax.ShapeDtypeStruct(shape, f32),
                jax.ShapeDtypeStruct((pair, stations * NTERM), f32),
            ),
            in_specs=[VM, VM, VM, SM, VM, VM, VM, VM, VM, SM],
            out_specs=(VM,) * 3,
            scratch_shapes=[
                pltpu.VMEM((8, 128), f32),
                pltpu.VMEM((n_dir,) + shape, f32),
                pltpu.VMEM((n_dir, 8, flat), f32),
                pltpu.VMEM((n_chan, 8, 128), f32),
                pltpu.VMEM((flat, 8), f32),
                pltpu.VMEM((flat, stations), f32),
                pltpu.VMEM((flat, stations), f32),
                pltpu.VMEM((stations, 2 * stations), f32),
                pltpu.VMEM((clusters, 8, stations), f32),
                pltpu.VMEM((pair, stations), f32),
                pltpu.VMEM((pair, stations), f32),
                pltpu.VMEM((n_chan, 8, small), f32),
                pltpu.VMEM((n_chan, 8, small), f32),
                pltpu.VMEM((pair, lanes), f32),
                pltpu.VMEM((n_dir, pair, lanes), f32),
                pltpu.VMEM((pair, lanes), f32),
                pltpu.VMEM((n_chan, pair, lanes), f32),
                dma((n_dir,)),
                dma((n_dir,)),
                dma((n_dir,)),
                dma((n_dir,)),
                dma((n_chan,)),
                dma((n_chan,)),
                dma((n_chan,)),
                dma((n_chan,)),
                dma((n_dir,)),
                dma((n_dir,)),
                dma((n_chan,)),
                dma((n_chan,)),
            ],
            compiler_params=pltpu.CompilerParams(collective_id=0, has_side_effects=True),
            name="calibrate",
        )(
            visibilities[0],
            station_uv,
            table,
            band_offset,
            gains_init,
            duals_init,
            poly,
            penalty.reshape(1, clusters),
            harmonics,
            threshold,
        )
        return gains, duals, consensus.reshape(2, clusters, stations * NTERM)

    return jax.shard_map(
        shards,
        mesh=mesh,
        in_specs=(
            P("chan", None, None, None),
            P(),
            P(None, "dir", None),
            P("dir", None),
            P("chan"),
            P(None, "dir", "chan", None),
            P(None, "dir", "chan", None),
            P(None, "dir", None),
            P("dir"),
            P(),
            P(),
        ),
        out_specs=(
            P(None, "dir", "chan", None),
            P(None, "dir", "chan", None),
            P(None, "dir", None),
        ),
        check_vma=False,
    )
```

time: 76 us -> 56.9 us (0.75)
  Pallas kernels: 63.6 us -> 49.6 us
  local copies, waits for them, and re-layouts: 9.31 us -> 4.38 us
    pallas_call x4 -> x1, Pallas kernels: 63.6 us -> 49.6 us  [shards(): pl.pallas_call(functools.partial(step_kernel, n_dir, n_chan, sources), ou...]
    unnamed x15 -> x7, local copies, waits for them, and re-layouts: 7.22 us -> 3.45 us
    broadcast_in_dim x2 -> x0, local copies, waits for them, and re-layouts: 1.18 us -> none  [the longest x1 0.59 us: shards(): cut = jnp.broadcast_to(threshold.reshape(1, 1), (8, 128))]
where the time goes in v1:
time: 56.9 us; the launch traced here: 56.6 us
  Pallas kernels  49.6 us (87%)
  local copies, waits for them, and re-layouts  4.38 us (8%)
  between operations  1.97 us (3%)
  other arithmetic  0.68 us (1%)
    pallas_call x1, Pallas kernels, shards(): pl.pallas_call(functools.partial(step_kernel, n_dir, n_chan, sources), ou...  49.6 us
    unnamed x7, local copies, waits for them, and re-layouts  3.45 us

profile of v1, /device:TPU:0, one launch (start us, length us, event | category | flops | bytes accessed | tf_op | source)
XLA Modules:
  0.0 56.6 jit_solution(10299842720575008564)
XLA Ops:
  0.6 0.0 copy-start.1
  2.0 0.1 pad.2.clone
  2.0 0.8 %reshape.22 = f32[1,512]{1,0:T(1,128)S(1)} reshape(f32[16,32]{1,0:T(8,128)} %param.14) | data formatting | bytes 4096 | tf_op jit(solution)/shard_map/reshape | solution.py:436
  2.8 0.0 copy-done.1
  2.8 0.1 reshape.21
  2.9 0.7 %maximum_maximum_fusion.table = f32[8,512]{1,0:T(8,128)} fusion(f32[1,512]{1,0:T(1,128)S(1)} %reshape.22, f32[2,512]{1,0:T(2,128)S(1)} %reshape.21, f32[8]{0:T(128)S(1)} %pad.2.clone), kind=kLoop, calls=%fused_computation | loop fusion | flops 8192 | bytes 22560 | tf_op jit(solution)/shard_map/concatenate | solution.py:433
  3.6 49.6 %calibrate.1 = (f32[2,16,1,256]{3,2,1,0:T(1,128)}, f32[2,16,1,256]{3,2,1,0:T(1,128)}, f32[32,1024]{1,0:T(8,128)}) custom-call(f32[256,2,256]{2,1,0:T(2,128)} %bitcast.4, f32[2,256]{1,0:T(2,128)} %uv.1, f32[8,512]{1,0:T(8,128)} %maximum_maximum_fusion.table, f32[1]{0:T(128)S(6)} %copy.17.band, f32[2,16,1,256]{3,2,1,0:T(1,128)} %g_ref.1, ...), custom_call_target="tpu_custom_call" | custom-call | tf_op jit(solution)/shard_map/calibrate/pallas_call | solution.py:445
  53.1 0.0 copy-start
  53.1 1.4 %copy.19 = f32[2,16,1,256]{3,2,1,0:T(1,128)} copy(f32[2,16,1,256]{3,2,1,0:T(1,128)} %get-tuple-element.12) | data formatting | bytes 65536
  54.5 1.4 %copy.20 = f32[2,16,1,256]{3,2,1,0:T(1,128)} copy(f32[2,16,1,256]{3,2,1,0:T(1,128)} %get-tuple-element.13) | data formatting | bytes 65536
  55.9 0.0 copy-done
  55.9 0.7 %copy.21 = f32[2,16,1024]{2,1,0:T(8,128)} copy(f32[2,16,1024]{2,1,0:T(8,128)S(1)} %bitcast.5) | data formatting | bytes 262144
  (1 shorter events, 0.0 us)
Async XLA Ops:
  0.6 2.2 %copy-start.1 = (f32[2,16,32]{2,1,0:T(8,128)S(1)}, f32[2,16,32]{2,1,0:T(8,128)}, u32[]{:S(2)}) copy-start(f32[2,16,32]{2,1,0:T(8,128)} %param.13) | copy-start | bytes 12292
  53.1 2.8 %copy-start = (f32[32,1024]{1,0:T(8,128)S(1)}, f32[32,1024]{1,0:T(8,128)}, u32[]{:S(2)}) copy-start(f32[32,1024]{1,0:T(8,128)} %get-tuple-element.8) | copy-start | bytes 393220

commit v2 on v1

--- a/solution.py
+++ b/solution.py
@@ -237,15 +237,20 @@
         e_r = er[pl.ds(start, sources), :]
         e_i = ei[pl.ds(start, sources), :]
         weight = src_t[pl.ds(start, sources), :][:, 2:3]
-        lh, ll = split(jnp.concatenate([e_r * weight, e_i * weight], axis=0))
+        left = jnp.concatenate([e_r * weight, e_i * weight], axis=0)
+        near = left.astype(jnp.bfloat16).astype(jnp.float32)
+        turned_left = jnp.transpose(jnp.concatenate([near, left - near], axis=0))
+        turned_left = turned_left.astype(jnp.bfloat16)
         rh, rl = split(
             jnp.concatenate(
                 [jnp.concatenate([e_r, e_i], axis=0), jnp.concatenate([-e_i, e_r], axis=0)],
                 axis=1,
             )
         )
-        coherency = tdot(
-            jnp.concatenate([lh, lh, ll], axis=0), jnp.concatenate([rh, rl, rh], axis=0)
+        coherency = jnp.dot(
+            jnp.concatenate([turned_left, turned_left], axis=1),
+            jnp.concatenate([rh, rh, rl, rl], axis=0),
+            preferred_element_type=jnp.float32,
         )
         c_r = coherency[:, :stations]
         c_i = coherency[:, stations:]
@@ -256,22 +261,26 @@
         b_i = r_i * c_r - r_r * c_i
         block = rows[k]
         g_r, g_i = block[0:1], block[1:2]
-        cols = jnp.transpose(block)
+        rho = block[4:5]
+        g_2 = g_r * g_r + g_i * g_i
+        cols = jnp.transpose(jnp.concatenate([block[0:2], g_2, block[3:8]], axis=0))
         k_r, k_i = cols[:, 0:1], cols[:, 1:2]
-        rho = cols[:, 4:5]
-        n_r = jnp.sum(b_r * g_r - b_i * g_i, axis=1, keepdims=True)
-        n_i = jnp.sum(b_r * g_i + b_i * g_r, axis=1, keepdims=True)
-        total = jnp.sum(power * (g_r * g_r + g_i * g_i), axis=1, keepdims=True)
+        n_r = jnp.sum(b_r * k_r + b_i * k_i, axis=0, keepdims=True)
+        n_i = jnp.sum(b_r * k_i - b_i * k_r, axis=0, keepdims=True)
+        total = jnp.sum(power * cols[:, 2:3], axis=0, keepdims=True)
         inverse = 1.0 / (total + rho)
-        h_r = (n_r + k_r * total + cols[:, 2:3]) * inverse
-        h_i = (n_i + k_i * total + cols[:, 3:4]) * inverse
-        mix_r = k_r * h_r + k_i * h_i
-        mix_i = k_r * h_i - k_i * h_r
-        m_r = jnp.sum(b_r * h_r + b_i * h_i, axis=0, keepdims=True)
-        m_i = jnp.sum(b_r * h_i - b_i * h_r, axis=0, keepdims=True)
-        t_0 = jnp.sum(power * mix_r, axis=0, keepdims=True)
-        t_1 = jnp.sum(power * mix_i, axis=0, keepdims=True)
-        t_2 = jnp.sum(power * (h_r * h_r + h_i * h_i), axis=0, keepdims=True)
+        h_r = (n_r + g_r * total + block[2:3]) * inverse
+        h_i = (n_i + g_i * total + block[3:4]) * inverse
+        mix_r = g_r * h_r + g_i * h_i
+        mix_i = g_r * h_i - g_i * h_r
+        h_2 = h_r * h_r + h_i * h_i
+        cols = jnp.transpose(jnp.concatenate([h_r, h_i, mix_r, mix_i, h_2, block[5:8]], axis=0))
+        q_r, q_i = cols[:, 0:1], cols[:, 1:2]
+        m_r = jnp.sum(b_r * q_r + b_i * q_i, axis=0, keepdims=True)
+        m_i = jnp.sum(b_r * q_i - b_i * q_r, axis=0, keepdims=True)
+        t_0 = jnp.sum(power * cols[:, 2:3], axis=0, keepdims=True)
+        t_1 = jnp.sum(power * cols[:, 3:4], axis=0, keepdims=True)
+        t_2 = jnp.sum(power * cols[:, 4:5], axis=0, keepdims=True)
         inverse = 1.0 / (t_2 + block[4:5])
         new_r = (m_r + g_r * t_0 - g_i * t_1 + block[2:3]) * inverse
         new_i = (m_i + g_r * t_1 + g_i * t_0 + block[3:4]) * inverse

time: 56.9 us -> 56.8 us (level)
  no operation moved by 1% of the time
where the time goes in v2:
time: 56.8 us; the launch traced here: 56.4 us
  Pallas kernels  49.4 us (87%)
  local copies, waits for them, and re-layouts  4.38 us (8%)
  between operations  1.97 us (3%)
  other arithmetic  0.68 us (1%)
    pallas_call x1, Pallas kernels, shards(): pl.pallas_call(functools.partial(step_kernel, n_dir, n_chan, sources), ou...  49.4 us
    unnamed x7, local copies, waits for them, and re-layouts  3.45 us

profile of v2, /device:TPU:0, one launch (start us, length us, event | category | flops | bytes accessed | tf_op | source)
XLA Modules:
  0.0 56.4 jit_solution(14014742503218065488)
XLA Ops:
  0.6 0.0 copy-start.1
  2.0 0.1 pad.2.clone
  2.0 0.8 %reshape.22 = f32[1,512]{1,0:T(1,128)S(1)} reshape(f32[16,32]{1,0:T(8,128)} %param.14) | data formatting | bytes 4096 | tf_op jit(solution)/shard_map/reshape | solution.py:445
  2.8 0.0 copy-done.1
  2.8 0.1 reshape.21
  2.9 0.7 %maximum_maximum_fusion.table = f32[8,512]{1,0:T(8,128)} fusion(f32[1,512]{1,0:T(1,128)S(1)} %reshape.22, f32[2,512]{1,0:T(2,128)S(1)} %reshape.21, f32[8]{0:T(128)S(1)} %pad.2.clone), kind=kLoop, calls=%fused_computation | loop fusion | flops 8192 | bytes 22560 | tf_op jit(solution)/shard_map/concatenate | solution.py:442
  3.6 49.4 %calibrate.1 = (f32[2,16,1,256]{3,2,1,0:T(1,128)}, f32[2,16,1,256]{3,2,1,0:T(1,128)}, f32[32,1024]{1,0:T(8,128)}) custom-call(f32[256,2,256]{2,1,0:T(2,128)} %bitcast.4, f32[2,256]{1,0:T(2,128)} %uv.1, f32[8,512]{1,0:T(8,128)} %maximum_maximum_fusion.table, f32[1]{0:T(128)S(6)} %copy.17.band, f32[2,16,1,256]{3,2,1,0:T(1,128)} %g_ref.1, ...), custom_call_target="tpu_custom_call" | custom-call | tf_op jit(solution)/shard_map/calibrate/pallas_call | solution.py:454
  53.0 0.0 copy-start
  53.0 1.4 %copy.19 = f32[2,16,1,256]{3,2,1,0:T(1,128)} copy(f32[2,16,1,256]{3,2,1,0:T(1,128)} %get-tuple-element.12) | data formatting | bytes 65536
  54.4 1.4 %copy.20 = f32[2,16,1,256]{3,2,1,0:T(1,128)} copy(f32[2,16,1,256]{3,2,1,0:T(1,128)} %get-tuple-element.13) | data formatting | bytes 65536
  55.8 0.0 copy-done
  55.8 0.7 %copy.21 = f32[2,16,1024]{2,1,0:T(8,128)} copy(f32[2,16,1024]{2,1,0:T(8,128)S(1)} %bitcast.5) | data formatting | bytes 262144
  (1 shorter events, 0.0 us)
Async XLA Ops:
  0.6 2.2 %copy-start.1 = (f32[2,16,32]{2,1,0:T(8,128)S(1)}, f32[2,16,32]{2,1,0:T(8,128)}, u32[]{:S(2)}) copy-start(f32[2,16,32]{2,1,0:T(8,128)} %param.13) | copy-start | bytes 12292
  53.0 2.8 %copy-start = (f32[32,1024]{1,0:T(8,128)S(1)}, f32[32,1024]{1,0:T(8,128)}, u32[]{:S(2)}) copy-start(f32[32,1024]{1,0:T(8,128)} %get-tuple-element.8) | copy-start | bytes 393220

commit v3 on v2

--- a/solution.py
+++ b/solution.py
@@ -290,7 +290,14 @@
         gains_out[1, k] = new_i
         return carry
 
-    lax.fori_loop(0, clusters, solve, 0)
+    batch = math.gcd(clusters, 2)
+
+    def solve_batch(b, carry):
+        for i in range(batch):
+            solve(b * batch + i, carry)
+        return carry
+
+    lax.fori_loop(0, clusters // batch, solve_batch, 0)
 
     spread = gains[...] + offset
     each = stations // n_chan
@@ -416,6 +423,12 @@
         dual_out[1, k] = fresh[clusters + k : clusters + k + 1]
 
 
+def emit_kernel(a, b, c, a_out, b_out, c_out):
+    a_out[...] = a[...]
+    b_out[...] = b[...]
+    c_out[...] = c[...]
+
+
 def solution(mesh):
     n_dir, n_chan = mesh.shape["dir"], mesh.shape["chan"]
 
@@ -505,6 +518,17 @@
             harmonics,
             threshold,
         )
+        gains, duals, consensus = pl.pallas_call(
+            emit_kernel,
+            out_shape=(
+                jax.ShapeDtypeStruct(shape, f32),
+                jax.ShapeDtypeStruct(shape, f32),
+                jax.ShapeDtypeStruct((pair, stations * NTERM), f32),
+            ),
+            in_specs=[VM] * 3,
+            out_specs=(VM,) * 3,
+            name="emit",
+        )(gains, duals, consensus)
         return gains, duals, consensus.reshape(2, clusters, stations * NTERM)
 
     return jax.shard_map(

time: 56.8 us -> 52.6 us (0.926)
  local copies, waits for them, and re-layouts: 4.38 us -> 0.94 us
  Pallas kernels: 49.4 us -> 48.8 us
    unnamed x7 -> x2, local copies, waits for them, and re-layouts: 3.45 us -> 0.01 us
    pallas_call x1, Pallas kernels: 49.4 us -> 47.2 us  [shards(): pl.pallas_call(functools.partial(step_kernel, n_dir, n_chan, sources), ou...]
    pallas_call x0 -> x1, Pallas kernels: none -> 1.65 us  [shards(): pl.pallas_call(emit_kernel, out_shape=(jax.ShapeDtypeStruct(shape, f32),...]
where the time goes in v3:
time: 52.6 us; the launch traced here: 52.4 us
  Pallas kernels  48.8 us (93%)
  between operations  1.96 us (4%)
  local copies, waits for them, and re-layouts  0.94 us (2%)
  other arithmetic  0.68 us (1%)
    pallas_call x1, Pallas kernels, shards(): pl.pallas_call(functools.partial(step_kernel, n_dir, n_chan, sources), ou...  47.2 us
    pallas_call x1, Pallas kernels, shards(): pl.pallas_call(emit_kernel, out_shape=(jax.ShapeDtypeStruct(shape, f32),...  1.65 us

profile of v3, /device:TPU:0, one launch (start us, length us, event | category | flops | bytes accessed | tf_op | source)
XLA Modules:
  0.0 52.4 jit_solution(7135211199854617845)
XLA Ops:
  0.6 0.0 copy-start
  2.0 0.1 pad.2.clone
  2.0 0.8 %reshape.22 = f32[1,512]{1,0:T(1,128)S(1)} reshape(f32[16,32]{1,0:T(8,128)} %param.14) | data formatting | bytes 4096 | tf_op jit(solution)/shard_map/reshape | solution.py:458
  2.8 0.0 copy-done
  2.8 0.1 reshape.21
  2.9 0.7 %maximum_maximum_fusion.table = f32[8,512]{1,0:T(8,128)} fusion(f32[1,512]{1,0:T(1,128)S(1)} %reshape.22, f32[2,512]{1,0:T(2,128)S(1)} %reshape.21, f32[8]{0:T(128)S(1)} %pad.2.clone), kind=kLoop, calls=%fused_computation | loop fusion | flops 8192 | bytes 22560 | tf_op jit(solution)/shard_map/concatenate | solution.py:455
  3.6 47.2 %calibrate.1 = (f32[2,16,1,256]{3,2,1,0:T(1,128)}, f32[2,16,1,256]{3,2,1,0:T(1,128)}, f32[32,1024]{1,0:T(8,128)}) custom-call(f32[256,2,256]{2,1,0:T(2,128)} %bitcast.4, f32[2,256]{1,0:T(2,128)} %uv.1, f32[8,512]{1,0:T(8,128)} %maximum_maximum_fusion.table, f32[1]{0:T(128)S(6)} %copy.14.band, f32[2,16,1,256]{3,2,1,0:T(1,128)} %g_ref.1, ...), custom_call_target="tpu_custom_call" | custom-call | tf_op jit(solution)/shard_map/calibrate/pallas_call | solution.py:467
  50.7 1.6 %emit.1 = (f32[2,16,1,256]{3,2,1,0:T(1,128)}, f32[2,16,1,256]{3,2,1,0:T(1,128)}, f32[32,1024]{1,0:T(8,128)}) custom-call(f32[2,16,1,256]{3,2,1,0:T(1,128)} %get-tuple-element.9.a, f32[2,16,1,256]{3,2,1,0:T(1,128)} %get-tuple-element.10.b, f32[32,1024]{1,0:T(8,128)} %get-tuple-element.11.c), custom_call_target="tpu_custom_call" | custom-call | tf_op jit(solution)/shard_map/emit/pallas_call | solution.py:521
  (1 shorter events, 0.0 us)
Async XLA Ops:
  0.6 2.2 %copy-start = (f32[2,16,32]{2,1,0:T(8,128)S(1)}, f32[2,16,32]{2,1,0:T(8,128)}, u32[]{:S(2)}) copy-start(f32[2,16,32]{2,1,0:T(8,128)} %param.13) | copy-start | bytes 12292
